TPU v7x, 128 devices: a whole 4x4x4 slice. The times are simulated.
128 devices in a mesh: tm: 16 (over z_lo, y, core), head: 8 (over z_hi, x).
Axes of the slice: x: 4, y: 4, z: 4 (z_hi: 2, z_lo: 2; z = z_hi * 2 + z_lo), core: 2. Of those that a mesh axis runs over, the one named last changes fastest.
Arguments:
- query_vectors: bfloat16 [16384, 4096], P('tm', 'head'), may hold values from -6 to 6
- key_vectors: bfloat16 [16384, 4096], P('tm', 'head'), may hold values from -0.125 to 0.125
- value_vectors: bfloat16 [16384, 4096], P('tm', 'head'), may hold values from -6 to 6
- grad_out: bfloat16 [16384, 4096], P('tm', 'head'), may hold values from -8 to 8
- out_weight: bfloat16 [4096, 4096], P('tm', 'head'), may hold values from -0.09375 to 0.09375
- periods: int32 [32], P('head'), may hold values from 1 to 128, as said below
- log_decay: float32 [32, 16384], P('head', 'tm'), may hold values from -0.1109375 to 0, as said below
Outputs:
- query_gradient: bfloat16 [16384, 4096], P('tm', 'head')
- key_gradient: bfloat16 [16384, 4096], P('tm', 'head')
- value_gradient: bfloat16 [16384, 4096], P('tm', 'head')
- grad_weight: float32 [4096, 4096], P('tm', 'head')
Inputs may be any that keep to these rules, and one draw needn't show every extreme that they name: `periods`: some head has period 1 and some head period 128. `log_decay`: Negative.
All inputs are finite; a program needn't handle non-finite values.
Results may differ from a plain program's by a relative error of at most 0.023.
Values may be sent and summed in bfloat16 or wider, within the bound.
A program may use at most 128 MiB of HBM per device.

v0:
```python
import jax
import jax.numpy as jnp
from jax import lax
from jax.sharding import PartitionSpec as P

DK = 128
BLK = 512


def prefix(value, axis, combine, identity, reverse):
    count, place = (lax.axis_size(axis), lax.axis_index(axis))
    everything = jax.tree.map(
        lambda part, kind: lax.all_gather(part.astype(kind), axis),
        value,
        (jnp.bfloat16, jnp.bfloat16),
    )
    start = jax.tree.map(
        lambda part, zero: jnp.broadcast_to(jnp.asarray(zero, part.dtype), part.shape),
        value,
        identity,
    )

    def turn(k, before):
        at = count - 1 - k if reverse else k
        reached = at > place if reverse else at < place
        new = combine(
            before, jax.tree.map(lambda part, own: part[at].astype(own.dtype), everything, value)
        )
        return jax.tree.map(lambda a, b: jnp.where(reached, a, b), new, before)

    return lax.fori_loop(0, count, turn, start)


def block_mask(cumul, update):
    span_len = cumul.shape[1]
    causal = jnp.arange(span_len)[:, None] >= jnp.arange(span_len)[None, :]
    spread = jnp.where(causal[None], cumul[:, :, None] - cumul[:, None, :], -jnp.inf)
    return jnp.exp(spread) * update[:, None, :]


def pair_weights(query_matrix, key_matrix, value_matrix, gradient_rows, cumul, update_rows):
    decay_mask = block_mask(cumul, update_rows)
    scores = jnp.einsum(
        "thk,shk->hts", query_matrix, key_matrix, preferred_element_type=jnp.float32
    )
    reversed_blocks = jnp.einsum(
        "thv,shv->hts", gradient_rows, value_matrix, preferred_element_type=jnp.float32
    )
    return (
        (scores * decay_mask).astype(jnp.bfloat16),
        (reversed_blocks * decay_mask).astype(jnp.bfloat16),
    )


def layer_output(query_matrix, value_matrix, projection_weight, cumul, state_start):
    within = jnp.einsum(
        "hts,shv->thv", projection_weight, value_matrix, preferred_element_type=jnp.float32
    )
    carried_state = jnp.einsum(
        "qml,mla->qma",
        query_matrix,
        state_start.astype(jnp.bfloat16),
        preferred_element_type=jnp.float32,
    )
    return (within + jnp.exp(cumul).T[:, :, None] * carried_state).astype(jnp.bfloat16)


def input_grads(
    query_matrix,
    key_matrix,
    value_matrix,
    gradient_rows,
    projection_weight,
    reversed_blocks,
    cumul,
    update_rows,
    state_start,
    finish,
):
    state_reduced = state_start.astype(jnp.bfloat16)
    carry_reduced = finish.astype(jnp.bfloat16)
    incoming_gradient = jnp.exp(cumul).T[:, :, None]
    outgoing_gradient = (update_rows * jnp.exp(cumul[:, -1][:, None] - cumul)).T[:, :, None]
    query_gradient = jnp.einsum(
        "gea,agq->egq", reversed_blocks, key_matrix, preferred_element_type=jnp.float32
    ) + incoming_gradient * jnp.einsum(
        "sba,bda->sbd", gradient_rows, state_reduced, preferred_element_type=jnp.float32
    )
    key_gradient = jnp.einsum(
        "rwy,wre->yre", reversed_blocks, query_matrix, preferred_element_type=jnp.float32
    ) + outgoing_gradient * jnp.einsum(
        "wqx,qgx->wqg", value_matrix, carry_reduced, preferred_element_type=jnp.float32
    )
    value_gradient = jnp.einsum(
        "kyp,ykb->pkb", projection_weight, gradient_rows, preferred_element_type=jnp.float32
    ) + outgoing_gradient * jnp.einsum(
        "imx,mxd->imd", key_matrix, carry_reduced, preferred_element_type=jnp.float32
    )
    return (
        query_gradient.astype(jnp.bfloat16),
        key_gradient.astype(jnp.bfloat16),
        value_gradient.astype(jnp.bfloat16),
    )


def combine_carry(earlier, later):
    return (earlier[0] * later[0], later[0][:, None, None] * earlier[1] + later[1])


def per_device(query_vectors, key_vectors, value_vectors, grad_out, out_weight, periods, log_decay):
    tok_rows = query_vectors.shape[0]
    head_count = periods.shape[0]
    block_count = tok_rows // BLK
    full_grad = lax.all_gather(grad_out, "head", axis=1, tiled=True)
    columns = full_grad
    grad_mixed = jnp.dot(
        columns,
        lax.all_gather(out_weight, "tm", axis=0, tiled=True),
        preferred_element_type=jnp.float32,
    ).astype(jnp.bfloat16)
    offset = lax.axis_index("tm") * tok_rows
    positions = offset + jnp.arange(tok_rows, dtype=jnp.int32)
    update = (positions[None, :] % periods[:, None] == 0).astype(jnp.float32)
    step_log = update * periods[:, None].astype(jnp.float32) * log_decay
    cumulative = jnp.cumsum(step_log.reshape(head_count, block_count, BLK), axis=2).transpose(
        1, 0, 2
    )
    updates = update.reshape(head_count, block_count, BLK).transpose(1, 0, 2)

    def blocked(tensor):
        return tensor.reshape(block_count, BLK, head_count, DK)

    query_blocks = blocked(query_vectors)
    key_blocks = blocked(key_vectors)
    value_blocks = blocked(value_vectors)
    grad_blocks = blocked(grad_mixed)
    zero_state = jnp.zeros((head_count, DK, DK), jnp.float32)

    def forward(running, section):
        key_matrix, value_matrix, cumul, update_rows = section
        block_total = cumul[:, -1]
        factor = update_rows * jnp.exp(block_total[:, None] - cumul)
        decay_scaled = (key_matrix.astype(jnp.float32) * factor.T[:, :, None]).astype(jnp.bfloat16)
        outer_product = jnp.einsum(
            "ptz,ptb->tzb", decay_scaled, value_matrix, preferred_element_type=jnp.float32
        )
        return (jnp.exp(block_total)[:, None, None] * running + outer_product, running)

    state_local, state_starts = lax.scan(
        forward, zero_state, (key_blocks, value_blocks, cumulative, updates)
    )

    def backward(carried_in, section):
        query_matrix, gradient_rows, cumul = section
        decay_scaled = (query_matrix.astype(jnp.float32) * jnp.exp(cumul).T[:, :, None]).astype(
            jnp.bfloat16
        )
        outer_product = jnp.einsum(
            "yop,yoj->opj", decay_scaled, gradient_rows, preferred_element_type=jnp.float32
        )
        return (jnp.exp(cumul[:, -1])[:, None, None] * carried_in + outer_product, carried_in)

    grad_local, grad_ends = lax.scan(
        backward, zero_state, (query_blocks, grad_blocks, cumulative), reverse=True
    )
    totals = cumulative[:, :, -1]
    shrink = jnp.exp(jnp.sum(totals, axis=0))
    identity = (jnp.ones((head_count,), jnp.float32), zero_state)
    _, state_in = prefix((shrink, state_local), "tm", combine_carry, identity, False)
    _, grad_in = prefix((shrink, grad_local), "tm", combine_carry, identity, True)
    running_sum = jnp.cumsum(totals, axis=0)
    before = running_sum - totals
    later_sum = jnp.sum(totals, axis=0)[None] - running_sum
    starts = jnp.exp(before)[:, :, None, None] * state_in[None] + state_starts
    finishes = jnp.exp(later_sum)[:, :, None, None] * grad_in[None] + grad_ends
    sections = (
        query_blocks,
        key_blocks,
        value_blocks,
        grad_blocks,
        cumulative,
        updates,
        starts,
        finishes,
    )

    def forward_output(section):
        query_matrix, key_matrix, value_matrix, gradient_rows, cumul, update_rows, state_start = (
            section
        )
        projection_weight, reversed_blocks = pair_weights(
            query_matrix, key_matrix, value_matrix, gradient_rows, cumul, update_rows
        )
        return (
            layer_output(query_matrix, value_matrix, projection_weight, cumul, state_start),
            projection_weight,
            reversed_blocks,
        )

    mixed, weight_blocks, backed_blocks = lax.map(forward_output, sections[:7])
    mixed_rows = mixed.reshape(tok_rows, head_count * DK)
    columns = full_grad
    grad_weight = lax.psum_scatter(
        lax.dot_general(
            columns, mixed_rows, (((0,), (0,)), ((), ())), preferred_element_type=jnp.float32
        ).astype(jnp.bfloat16),
        "tm",
        scatter_dimension=0,
        tiled=True,
    ).astype(jnp.float32)

    def gradient_output(section):
        (
            query_matrix,
            key_matrix,
            value_matrix,
            gradient_rows,
            cumul,
            update_rows,
            state_start,
            finish,
            projection_weight,
            reversed_blocks,
        ) = section
        return input_grads(
            query_matrix,
            key_matrix,
            value_matrix,
            gradient_rows,
            projection_weight,
            reversed_blocks,
            cumul,
            update_rows,
            state_start,
            finish,
        )

    query_gradient, key_gradient, value_gradient = lax.map(
        gradient_output, sections + (weight_blocks, backed_blocks)
    )
    return (
        query_gradient.reshape(tok_rows, head_count * DK),
        key_gradient.reshape(tok_rows, head_count * DK),
        value_gradient.reshape(tok_rows, head_count * DK),
        grad_weight,
    )


def solution(mesh):
    return jax.shard_map(
        per_device,
        mesh=mesh,
        in_specs=(
            P("tm", "head"),
            P("tm", "head"),
            P("tm", "head"),
            P("tm", "head"),
            P("tm", "head"),
            P("head"),
            P("head", "tm"),
        ),
        out_specs=(P("tm", "head"), P("tm", "head"), P("tm", "head"), P("tm", "head")),
        check_vma=False,
    )
```

profile of v0, /device:TPU:6, one launch (start us, length us, event | category | flops | bytes accessed | tf_op | source)
XLA Modules:
  0.0 386.0 jit_solution(7410916782412862764)
XLA Ops:
  11.3 2.4 reduce-window.6
  21.0 5.9 %fusion.90 = f32[2,4,512]{1,2,0:T(8,128)} fusion(s32[4]{0:T(128)S(1)} %get-tuple-element.848, s32[2,512]{1,0:T(2,128)S(1)} %add_add_fusion, pred[4]{0:T(512)(128)(4,1)S(1)} %broadcast_compare_fusion), kind=kLoop, calls=%fused_computation.136 | loop fusion | flops 36864 | bytes 20500 | tf_op jit(solution)/shard_map/convert_element_type | solution.py:123
  27.8 4.4 %while.90 = (s32[]{:T(128)}, f32[4,128,128]{2,1,0:T(8,128)S(1)}, f32[2,4,128,128]{3,2,1,0:T(8,128)}, f32[2,4,512]{1,2,0:T(8,128)S(1)}, bf16[2,512,4,128]{1,3,2,0...) while((s32[]{:T(128)}, f32[4,128,128]{2,1,0:T(8,128)S(1)}, ...), condition=%wide.region_5.6_spmd.clone, body=%wide.region_4.5_spmd.clone.sunk | while | flops 68161536 | bytes 2164928 | solution.py:149
  37.2 31.3 %all-reduce = bf16[64]{0:T(256)(128)(2,1)S(1)} all-reduce(bf16[64]{0:T(256)(128)(2,1)S(1)} %dynamic-update-slice), channel_id=2, replica_groups=mesh['tm'=16,'head'=8] {'tm'}, use_global_device_ids=true, to_apply=%add | all-reduce | flops 64 | bytes 256
  68.6 2.2 reshape.185
  70.8 2.5 copy.84
  73.4 97.4 %all-gather.8.cloned.1.call-done = bf16[1024,4096]{1,0:T(8,128)(2,1)} async-done(((bf16[1024,512]{1,0:T(8,128)(2,1)}), bf16[1024,4096]{1,0:T(8,128)(2,1)}) %all-gather.8.cloned.1.call-update) | async-done | bytes 8388624 | tf_op jit(solution)/shard_map/all_gather | solution.py:114
  170.8 10.0 %convolution_convert_fusion.1 = bf16[1024,512]{1,0:T(8,128)(2,1)} fusion(bf16[1024,4096]{1,0:T(8,128)(2,1)} %all-gather.8.cloned.1.call-done, bf16[4096,512]{1,0:T(8,128)(2,1)} %all-gather.10.cloned.1.call-done), kind=kOutput, calls=%fused_computation.123 | convolution fusion | flops 4295491584 | bytes 13631488 | tf_op jit(solution)/shard_map/dot_general | solution.py:116
  185.1 7.2 %while.92 = (s32[]{:T(128)}, f32[4,128,128]{2,1,0:T(8,128)S(1)}, f32[2,4,128,128]{3,2,1,0:T(8,128)}, f32[2,4,512]{1,2,0:T(8,128)S(1)}, bf16[2,512,4,128]{1,3,2,0...) while((s32[]{:T(128)}, f32[4,128,128]{2,1,0:T(8,128)S(1)}, ...), condition=%wide.region_9.10_spmd.clone, body=%wide.region_8.9_spmd.clone.sunk | while | flops 68157440 | bytes 2148499 | solution.py:163
  193.2 11.9 %all-gather.12.cloned.1.call-done = bf16[64,128,128]{2,1,0:T(8,128)(2,1)} async-done(((bf16[4,128,128]{2,1,0:T(8,128)(2,1)}), bf16[64,128,128]{2,1,0:T(8,128)(2,1)}) %all-gather.12.cloned.1.call-update) | async-done | bytes 2097168 | tf_op jit(solution)/shard_map/all_gather | solution.py:13
  205.1 28.6 %while.91 = (s32[]{:T(128)}, f32[4,128,128]{2,1,0:T(8,128)}, s32[]{:T(128)}, bf16[16,4]{1,0:T(8,128)(2,1)S(1)}, bf16[16,4,128,128]{3,2,1,0:T(8,128)(2,1)}, /*index=5*/s32[]{:T(128)}, s32[]{:T(128)}) while((s32[]{:T(128)}, f32[4,128,128]{2,1,0:T(8,128)}, s32[]{:T(128)}, bf16[16,4]{1,0:T(8,128)(2,1)S(1)}, ...), condition=%wide.region_7.8_spmd.clone, body=%wide.region_6.7_spmd.clone.sunk | while | flops 327688 | bytes 655505 | solution.py:31
  233.7 7.0 %all-gather.14.cloned.1.call-done = bf16[64,128,128]{2,1,0:T(8,128)(2,1)} async-done(((bf16[4,128,128]{2,1,0:T(8,128)(2,1)}), bf16[64,128,128]{2,1,0:T(8,128)(2,1)}) %all-gather.14.cloned.1.call-update) | async-done | bytes 2097168 | tf_op jit(solution)/shard_map/all_gather | solution.py:13
  240.7 17.0 %while.93 = (s32[]{:T(128)}, f32[4,128,128]{2,1,0:T(8,128)S(1)}, s32[]{:T(128)}, bf16[16,4]{1,0:T(8,128)(2,1)S(1)}, bf16[16,4,128,128]{3,2,1,0:T(8,128)(2,1)}, /*index=5*/s32[]{:T(128)}, s32[]{:T(128)}, s32[]{:T(128)}, s32[]{:T(128)}) while((s32[]{:T(128)}, f32[4,128,128]{2,1,0:T(8,128)S(1)}, s32[]{:T(128)}, ...), condition=%wide.region_11.12_spmd.clone, body=%wide.region_10.11_spmd.clone.sunk | while | flops 327692 | bytes 655567 | solution.py:31
  261.1 38.4 %while.88 = (s32[]{:T(128)}, bf16[2,512,4,128]{3,2,1,0:T(4,128)(2,1)}, bf16[2,4,512,512]{3,2,1,0:T(8,128)(2,1)}, bf16[2,4,512,512]{3,2,1,0:T(8,128)(2,1)}, bf16[...) while((s32[]{:T(128)}, ...), condition=%wide.region_13.14_spmd, body=%wide.region_12.13_spmd.sunk | while | flops 883949568 | bytes 30411028 | solution.py:200
  264.3 2.9 bitcast_dynamic-update-slice_fusion.8
  268.5 2.6 convolution_bitcast_fusion.6
  272.1 2.2 fusion.140
  276.7 3.6 bitcast_dynamic-update-slice_fusion.9
  283.5 2.9 bitcast_dynamic-update-slice_fusion.8
  287.7 2.6 convolution_bitcast_fusion.6
  295.9 3.6 bitcast_dynamic-update-slice_fusion.9
  299.5 10.2 %fusion.86 = bf16[4096,512]{0,1:T(8,128)(2,1)} fusion(bf16[1024,4096]{1,0:T(8,128)(2,1)} %all-gather.8.cloned.1.call-done, bf16[128,8,4,128]{3,2,1,0:T(4,128)(2,1)} %bitcast.351), kind=kOutput, calls=%fused_computation.122 | convolution fusion | flops 4297064448 | bytes 13631488 | tf_op jit(solution)/shard_map/dot_general | solution.py:204
  313.5 39.7 %while.89 = (s32[]{:T(128)}, bf16[2,512,4,128]{3,2,1,0:T(4,128)(2,1)}, bf16[2,512,4,128]{3,2,1,0:T(4,128)(2,1)}, bf16[2,512,4,128]{3,2,1,0:T(4,128)(2,1)}, bf16[...) while((s32[]{:T(128)}, ...), condition=%wide.region_15.16_spmd, body=%wide.region_14.15_spmd.sunk | while | flops 1008996352 | bytes 24100036 | solution.py:238
  315.6 2.2 fusion.153
  320.4 2.4 fusion.156
  326.3 2.4 constant_dynamic-update-slice_fusion.8
  335.5 2.2 fusion.153
  340.2 2.4 fusion.156
  346.1 2.4 constant_dynamic-update-slice_fusion.8
  353.2 2.5 copy.128
  355.6 2.4 copy.129
  359.2 18.3 %reduce-scatter.2.cloned.1.call-done = bf16[256,512]{0,1:T(8,128)(2,1)} async-done(((bf16[4096,512]{0,1:T(8,128)(2,1)}), bf16[256,512]{0,1:T(8,128)(2,1)}) %reduce-scatter.2.cloned.1.call-update) | async-done | bytes 262160 | tf_op jit(solution)/shard_map/reduce_scatter | solution.py:203
  (221 shorter events, 131.8 us)
Async XLA Ops:
  7.2 66.2 %all-gather.10.cloned.1.call-start = ((), (), s32[]{:S(2)}) async-start(), calls=%async_computation.2 | async-start | bytes 4456448 | tf_op jit(solution)/shard_map/all_gather | solution.py:118
  7.9 162.9 %all-gather.8.cloned.1.call-start = ((), (), s32[]{:S(2)}) async-start(), calls=%async_computation.1 | async-start | bytes 9437184 | tf_op jit(solution)/shard_map/all_gather | solution.py:114
  8.6 196.5 %all-gather.12.cloned.1.call-start = ((), (), s32[]{:S(2)}) async-start(), calls=%async_computation.4 | async-start | bytes 2228224 | tf_op jit(solution)/shard_map/all_gather | solution.py:13
  16.3 1.0 copy-start.3
  27.8 8.0 %copy-start.10 = (u32[128]{0:T(128)S(1)}, u32[128]{0:T(128)}, u32[]{:S(2)}) copy-start(u32[128]{0:T(128)} %constant.190) | copy-start | bytes 1540
  32.2 148.6 %copy-start.2 = (bf16[2,512,4,128]{3,1,2,0:T(8,128)(2,1)}, bf16[2,512,4,128]{3,1,2,0:T(8,128)(2,1)S(1)}, u32[]{:S(2)}) copy-start(bf16[2,512,4,128]{3,1,2,0:T(8,128)(2,1)S(1)} %get-tuple-element.1360) | copy-start | bytes 3145732
  33.0 207.8 %all-gather.14.cloned.1.call-start = ((), (), s32[]{:S(2)}) async-start(), calls=%async_computation.5 | async-start | bytes 2228224 | tf_op jit(solution)/shard_map/all_gather | solution.py:13
  192.4 67.5 %copy-start = (f32[2,4,512]{1,2,0:T(8,128)}, f32[2,4,512]{1,2,0:T(8,128)S(1)}, u32[]{:S(2)}) copy-start(f32[2,4,512]{1,2,0:T(8,128)S(1)} %get-tuple-element.1359) | copy-start | bytes 49156
  193.1 64.6 %copy-start.8 = (f32[2,4,128,128]{3,2,1,0:T(8,128)S(1)}, f32[2,4,128,128]{3,2,1,0:T(8,128)}, u32[]{:S(2)}) copy-start(f32[2,4,128,128]{3,2,1,0:T(8,128)} %get-tuple-element.530) | copy-start | bytes 1572868
  193.1 184.4 %reduce-scatter.2.cloned.1.call-start = ((), (), s32[]{:S(2)}) async-start(), calls=%async_computation.3 | async-start | bytes 4456448 | tf_op jit(solution)/shard_map/reduce_scatter | solution.py:203
  262.7 1.6 copy-start.1
  264.1 3.0 copy-start.9
  264.2 3.0 copy-start.5
  264.2 2.9 copy-start.4
  272.1 4.6 %copy-start.6 = (pred[512,512]{1,0:T(8,128)(4,1)S(1)}, pred[512,512]{1,0:T(8,128)(4,1)}, u32[]{:S(2)}) copy-start(pred[512,512]{1,0:T(8,128)(4,1)} %copy-done.5) | copy-start | bytes 786436 | tf_op jit(solution)/shard_map/while
  281.9 1.6 copy-start.1
  283.3 3.0 copy-start.9
  283.4 3.0 copy-start.5
  283.4 2.9 copy-start.4
  291.3 4.6 %copy-start.6 = (pred[512,512]{1,0:T(8,128)(4,1)S(1)}, pred[512,512]{1,0:T(8,128)(4,1)}, u32[]{:S(2)}) copy-start(pred[512,512]{1,0:T(8,128)(4,1)} %copy-done.5) | copy-start | bytes 786436 | tf_op jit(solution)/shard_map/while
  353.2 4.9 %copy-start.7 = (bf16[2,512,4,128]{3,2,1,0:T(4,128)(2,1)S(1)}, bf16[2,512,4,128]{3,2,1,0:T(4,128)(2,1)}, u32[]{:S(2)}) copy-start(bf16[2,512,4,128]{3,2,1,0:T(4,128)(2,1)} %get-tuple-element.532) | copy-start | bytes 3145732
Sparse Core Ops, SparseCore 0:
  9.7 39.5 all-gather.9
  51.5 119.2 all-gather.7
  172.5 32.5 all-gather.11
  206.7 33.9 all-gather.13
  309.9 67.6 reduce-scatter.1
where the time goes:
time: 389 us; the launch traced here: 386 us
  waiting for transfers between devices  136 us (35%)
  matrix products  69.1 us (18%)
  other arithmetic  67.4 us (17%)
  local copies, waits for them, and re-layouts  66.2 us (17%)
  blocking collectives  31.3 us (8%)
  between operations  14.6 us (4%)
    all_gather x1, waiting for transfers between devices, per_device(): full_grad = lax.all_gather(grad_out, 'head', axis=1, tiled=True)  97.4 us
    select_n x32, other arithmetic, turn(): return jax.tree.map(lambda a, b: jnp.where(reached, a, b), new, before)  44.7 us
    unnamed x1, blocking collectives  31.3 us
    all_gather x2, waiting for transfers between devices, prefix(): lax.all_gather(part.astype(kind), axis)  18.9 us
    reduce_scatter x1, waiting for transfers between devices, per_device(): lax.psum_scatter(lax.dot_general(columns, mixed_rows, (((0,), (0,)), ((),...  18.3 us
    dynamic_update_slice x14, local copies, waits for them, and re-layouts, per_device(): mixed, weight_blocks, backed_blocks = lax.map(forward_output, sections[:7])  16.9 us
    dot_general x1, matrix products, per_device(): lax.dot_general(columns, mixed_rows, (((0,), (0,)), ((), ())), preferred_...  10.2 us
    dot_general x1, matrix products, per_device(): jnp.dot(columns, lax.all_gather(out_weight, 'tm', axis=0, tiled=True), pr...  10 us
  transfers between devices with their start and end apart: 5, of which 4 were waited for; matrix products, arithmetic and copies ran while one was open for 34% of the time, Pallas kernels for 0%

commit v1 on v0

--- a/solution.py
+++ b/solution.py
@@ -111,7 +111,8 @@
     tok_rows = query_vectors.shape[0]
     head_count = periods.shape[0]
     block_count = tok_rows // BLK
-    full_grad = lax.all_gather(grad_out, "head", axis=1, tiled=True)
+    sent = jnp.stack([grad_out] * lax.axis_size("head"))
+    full_grad = jnp.concatenate(lax.all_to_all(sent, "head", 0, 0), axis=1)
     columns = full_grad
     grad_mixed = jnp.dot(
         columns,

time: 389 us -> 352 us (0.905)
  waiting for transfers between devices: 136 us -> 89 us
  starting transfers between devices: 0.2 us -> 8.34 us
  local copies, waits for them, and re-layouts: 66.2 us -> 71 us
    all_gather x1 -> x0, waiting for transfers between devices: 97.4 us -> none  [per_device(): full_grad = lax.all_gather(grad_out, 'head', axis=1, tiled=True)]
    all_to_all x0 -> x1, waiting for transfers between devices: none -> 63.7 us  [per_device(): full_grad = jnp.concatenate(lax.all_to_all(sent, 'head', 0, 0), axis=1)]
    all_gather x2, waiting for transfers between devices: 18.9 us -> 6.29 us  [prefix(): lax.all_gather(part.astype(kind), axis)]
    all_to_all x0 -> x1, starting transfers between devices: none -> 8.22 us  [per_device(): full_grad = jnp.concatenate(lax.all_to_all(sent, 'head', 0, 0), axis=1)]
    another operation x7 -> x8, local copies, waits for them, and re-layouts: 6.87 us -> 11.2 us
    unnamed x20 -> x27, local copies, waits for them, and re-layouts: 9.71 us -> 11.2 us
  transfers between devices with their start and end apart: 5 -> 5, of which waited for: 4 -> 3; matrix products, arithmetic and copies ran while one was open for 34% -> 39% of each run, Pallas kernels for 0% -> 0%
where the time goes in v1:
time: 352 us; the launch traced here: 349 us
  waiting for transfers between devices  89 us (25%)
  local copies, waits for them, and re-layouts  71 us (20%)
  matrix products  69.3 us (20%)
  other arithmetic  65.2 us (19%)
  blocking collectives  30.5 us (9%)
  between operations  14.6 us (4%)
  starting transfers between devices  8.34 us (2%)
    all_to_all x1, waiting for transfers between devices, per_device(): full_grad = jnp.concatenate(lax.all_to_all(sent, 'head', 0, 0), axis=1)  63.7 us
    select_n x32, other arithmetic, turn(): return jax.tree.map(lambda a, b: jnp.where(reached, a, b), new, before)  44.6 us
    unnamed x1, blocking collectives  30.5 us
    reduce_scatter x1, waiting for transfers between devices, per_device(): lax.psum_scatter(lax.dot_general(columns, mixed_rows, (((0,), (0,)), ((),...  18.2 us
    dynamic_update_slice x14, local copies, waits for them, and re-layouts, per_device(): mixed, weight_blocks, backed_blocks = lax.map(forward_output, sections[:7])  16.9 us
    unnamed x27, local copies, waits for them, and re-layouts  11.2 us
    dot_general x1, matrix products, per_device(): lax.dot_general(columns, mixed_rows, (((0,), (0,)), ((), ())), preferred_...  10.3 us
    dot_general x1, matrix products, per_device(): jnp.dot(columns, lax.all_gather(out_weight, 'tm', axis=0, tiled=True), pr...  10.2 us
  transfers between devices with their start and end apart: 5, of which 3 were waited for; matrix products, arithmetic and copies ran while one was open for 39% of the time, Pallas kernels for 0%

profile of v1, /device:TPU:6, one launch (start us, length us, event | category | flops | bytes accessed | tf_op | source)
XLA Modules:
  0.0 348.9 jit_solution(15012245707286951665)
XLA Ops:
  9.4 4.3 %stack.2 = bf16[8,1024,512]{1,2,0:T(8,128)(2,1)} broadcast(bf16[1024,512]{0,1:T(8,128)(2,1)S(1)} %copy.74), dimensions={1,2} | broadcast | bytes 9437184 | tf_op jit(solution)/shard_map/stack | solution.py:114
  13.7 8.2 %all-to-all-start = ((bf16[8,1024,512]{1,2,0:T(8,128)(2,1)}), bf16[8,1024,512]{1,2,0:T(8,128)(2,1)}, u32[]{:S(2)}, u32[]{:S(2)}) async-start(bf16[8,1024,512]{1,2,0:T(8,128)(2,1)} %stack.2), calls=%async_computation | async-start | bytes 16777216 | tf_op jit(solution)/shard_map/all_to_all | solution.py:115
  22.4 2.4 reduce-window.6
  31.1 5.9 %fusion.90 = f32[2,4,512]{1,2,0:T(8,128)} fusion(s32[4]{0:T(128)S(1)} %get-tuple-element.848, s32[2,512]{1,0:T(2,128)S(1)} %add_add_fusion, pred[4]{0:T(512)(128)(4,1)S(1)} %broadcast_compare_fusion), kind=kLoop, calls=%fused_computation.136 | loop fusion | flops 36864 | bytes 20500 | tf_op jit(solution)/shard_map/convert_element_type | solution.py:124
  37.9 4.4 %while.90 = (s32[]{:T(128)}, f32[4,128,128]{2,1,0:T(8,128)S(1)}, f32[2,4,128,128]{3,2,1,0:T(8,128)}, f32[2,4,512]{1,2,0:T(8,128)S(1)}, bf16[2,512,4,128]{1,3,2,0...) while((s32[]{:T(128)}, f32[4,128,128]{2,1,0:T(8,128)S(1)}, ...), condition=%wide.region_5.6_spmd.clone, body=%wide.region_4.5_spmd.clone.sunk | while | flops 68161536 | bytes 2164928 | solution.py:150
  47.3 30.5 %all-reduce = bf16[64]{0:T(256)(128)(2,1)S(1)} all-reduce(bf16[64]{0:T(256)(128)(2,1)S(1)} %dynamic-update-slice), channel_id=2, replica_groups=mesh['tm'=16,'head'=8] {'tm'}, use_global_device_ids=true, to_apply=%add | all-reduce | flops 64 | bytes 256
  80.0 2.4 copy.86
  82.5 63.7 %all-to-all-done = bf16[8,1024,512]{1,2,0:T(8,128)(2,1)} async-done(((bf16[8,1024,512]{1,2,0:T(8,128)(2,1)}), bf16[8,1024,512]{1,2,0:T(8,128)(2,1)}, u32[]{:S(2)}, u32[]{:S(2)}) %all-to-all-start) | async-done | bytes 8388640 | tf_op jit(solution)/shard_map/all_to_all | solution.py:115
  146.2 10.2 %convolution_convert_fusion.1 = bf16[1024,512]{1,0:T(8,128)(2,1)} fusion(bf16[1024,4096]{0,1:T(8,128)(2,1)} %bitcast.42, bf16[4096,512]{1,0:T(8,128)(2,1)} %all-gather.7.cloned.1.call-done), kind=kOutput, calls=%fused_computation.123 | convolution fusion | flops 4295491584 | bytes 13631488 | tf_op jit(solution)/shard_map/dot_general | solution.py:117
  156.4 2.2 reshape.198
  160.8 7.2 %while.92 = (s32[]{:T(128)}, f32[4,128,128]{2,1,0:T(8,128)S(1)}, f32[2,4,128,128]{3,2,1,0:T(8,128)}, f32[2,4,512]{1,2,0:T(8,128)S(1)}, bf16[2,512,4,128]{1,3,2,0...) while((s32[]{:T(128)}, f32[4,128,128]{2,1,0:T(8,128)S(1)}, ...), condition=%wide.region_9.10_spmd.clone, body=%wide.region_8.9_spmd.clone.sunk | while | flops 68157440 | bytes 2148499 | solution.py:164
  168.9 28.6 %while.91 = (s32[]{:T(128)}, f32[4,128,128]{2,1,0:T(8,128)}, s32[]{:T(128)}, bf16[16,4]{1,0:T(8,128)(2,1)S(1)}, bf16[16,4,128,128]{3,2,1,0:T(8,128)(2,1)}, /*index=5*/s32[]{:T(128)}, s32[]{:T(128)}) while((s32[]{:T(128)}, f32[4,128,128]{2,1,0:T(8,128)}, s32[]{:T(128)}, bf16[16,4]{1,0:T(8,128)(2,1)S(1)}, ...), condition=%wide.region_7.8_spmd.clone, body=%wide.region_6.7_spmd.clone.sunk | while | flops 327688 | bytes 655505 | solution.py:31
  197.5 6.3 %all-gather.11.cloned.1.call-done = bf16[64,128,128]{2,1,0:T(8,128)(2,1)} async-done(((bf16[4,128,128]{2,1,0:T(8,128)(2,1)}), bf16[64,128,128]{2,1,0:T(8,128)(2,1)}) %all-gather.11.cloned.1.call-update) | async-done | bytes 2097168 | tf_op jit(solution)/shard_map/all_gather | solution.py:13
  203.7 17.0 %while.93 = (s32[]{:T(128)}, f32[4,128,128]{2,1,0:T(8,128)S(1)}, s32[]{:T(128)}, bf16[16,4]{1,0:T(8,128)(2,1)S(1)}, bf16[16,4,128,128]{3,2,1,0:T(8,128)(2,1)}, /*index=5*/s32[]{:T(128)}, s32[]{:T(128)}, s32[]{:T(128)}, s32[]{:T(128)}) while((s32[]{:T(128)}, f32[4,128,128]{2,1,0:T(8,128)S(1)}, s32[]{:T(128)}, ...), condition=%wide.region_11.12_spmd.clone, body=%wide.region_10.11_spmd.clone.sunk | while | flops 327692 | bytes 655567 | solution.py:31
  224.1 38.4 %while.88 = (s32[]{:T(128)}, bf16[2,512,4,128]{3,2,1,0:T(4,128)(2,1)}, bf16[2,4,512,512]{3,2,1,0:T(8,128)(2,1)}, bf16[2,4,512,512]{3,2,1,0:T(8,128)(2,1)}, bf16[...) while((s32[]{:T(128)}, ...), condition=%wide.region_13.14_spmd, body=%wide.region_12.13_spmd.sunk | while | flops 883949568 | bytes 30411028 | solution.py:201
  227.2 2.9 bitcast_dynamic-update-slice_fusion.8
  231.5 2.6 convolution_bitcast_fusion.6
  239.6 3.6 %bitcast_dynamic-update-slice_fusion.9 = bf16[2,4,512,512]{3,2,1,0:T(8,128)(2,1)} fusion(bf16[2,4,512,512]{3,2,1,0:T(8,128)(2,1)} %get-tuple-element.1284, s32[]{:T(128)} %get-tuple-element.1281, f32[4,512]{1,0:T(4,128)} %copy-done.10, f32[4,512]{1,0:T(4,128)S(1)} %get-tuple-element.1121, pred[512,512]{1,0:T(8,128)(4,1)S(1)} %copy-done.6, ...), kind=kOutput, calls=%fused_computation.3.clone.1 | convolution fusion | flops 273678336 | bytes 3433472 | tf_op jit(solution)/shard_map/while/body/eval_jaxpr/thv,shv->hts/dot_general | solution.py:46
  246.4 2.9 bitcast_dynamic-update-slice_fusion.8
  250.7 2.6 convolution_bitcast_fusion.6
  258.8 3.7 %bitcast_dynamic-update-slice_fusion.9 = bf16[2,4,512,512]{3,2,1,0:T(8,128)(2,1)} fusion(bf16[2,4,512,512]{3,2,1,0:T(8,128)(2,1)} %get-tuple-element.1284, s32[]{:T(128)} %get-tuple-element.1281, f32[4,512]{1,0:T(4,128)} %copy-done.10, f32[4,512]{1,0:T(4,128)S(1)} %get-tuple-element.1121, pred[512,512]{1,0:T(8,128)(4,1)S(1)} %copy-done.6, ...), kind=kOutput, calls=%fused_computation.3.clone.1 | convolution fusion | flops 273678336 | bytes 3433472 | tf_op jit(solution)/shard_map/while/body/eval_jaxpr/thv,shv->hts/dot_general | solution.py:46
  262.5 10.3 %fusion.86 = bf16[4096,512]{0,1:T(8,128)(2,1)} fusion(bf16[1024,4096]{0,1:T(8,128)(2,1)} %bitcast.42, bf16[128,8,4,128]{3,2,1,0:T(4,128)(2,1)} %bitcast.354), kind=kOutput, calls=%fused_computation.122 | convolution fusion | flops 4297064448 | bytes 13631488 | tf_op jit(solution)/shard_map/dot_general | solution.py:205
  276.6 39.7 %while.89 = (s32[]{:T(128)}, bf16[2,512,4,128]{3,2,1,0:T(4,128)(2,1)}, bf16[2,512,4,128]{3,2,1,0:T(4,128)(2,1)}, bf16[2,512,4,128]{3,2,1,0:T(4,128)(2,1)}, bf16[...) while((s32[]{:T(128)}, ...), condition=%wide.region_15.16_spmd, body=%wide.region_14.15_spmd.sunk | while | flops 1008996352 | bytes 24100036 | solution.py:239
  278.7 2.2 fusion.153
  283.5 2.4 fusion.156
  289.4 2.4 constant_dynamic-update-slice_fusion.8
  298.6 2.2 fusion.153
  303.3 2.4 fusion.156
  309.2 2.4 constant_dynamic-update-slice_fusion.8
  316.3 2.5 copy.130
  318.8 2.4 copy.131
  322.3 18.2 %reduce-scatter.2.cloned.1.call-done = bf16[256,512]{0,1:T(8,128)(2,1)} async-done(((bf16[4096,512]{0,1:T(8,128)(2,1)}), bf16[256,512]{0,1:T(8,128)(2,1)}) %reduce-scatter.2.cloned.1.call-update) | async-done | bytes 262160 | tf_op jit(solution)/shard_map/reduce_scatter | solution.py:204
  (228 shorter events, 131.5 us)
Async XLA Ops:
  7.2 139.1 %all-gather.7.cloned.1.call-start = ((), (), s32[]{:S(2)}) async-start(), calls=%async_computation.2 | async-start | bytes 4456448 | tf_op jit(solution)/shard_map/all_gather | solution.py:119
  13.7 8.2 %copy-start.12 = (s32[4]{0:T(128)S(1)}, s32[4]{0:T(128)}, u32[]{:S(2)}) copy-start(s32[4]{0:T(128)} %param.24) | copy-start | bytes 52
  13.7 8.3 %copy-start.11 = (f32[4,1024]{1,0:T(4,128)S(1)}, f32[4,1024]{1,0:T(4,128)}, u32[]{:S(2)}) copy-start(f32[4,1024]{1,0:T(4,128)} %param.25) | copy-start | bytes 49156
  13.7 12.4 %copy-start.9 = (bf16[1024,512]{1,0:T(8,128)(2,1)S(1)}, bf16[1024,512]{1,0:T(8,128)(2,1)}, u32[]{:S(2)}) copy-start(bf16[1024,512]{1,0:T(8,128)(2,1)} %param.21) | copy-start | bytes 3145732
  13.7 132.5 %all-to-all-start = ((bf16[8,1024,512]{1,2,0:T(8,128)(2,1)}), bf16[8,1024,512]{1,2,0:T(8,128)(2,1)}, u32[]{:S(2)}, u32[]{:S(2)}) async-start(bf16[8,1024,512]{1,2,0:T(8,128)(2,1)} %stack.2), calls=%async_computation | async-start | bytes 16777216 | tf_op jit(solution)/shard_map/all_to_all | solution.py:115
  21.9 147.0 %all-gather.9.cloned.1.call-start = ((), (), s32[]{:S(2)}) async-start(), calls=%async_computation.4 | async-start | bytes 2228224 | tf_op jit(solution)/shard_map/all_gather | solution.py:13
  26.4 1.0 copy-start.3
  37.9 7.9 %copy-start.13 = (u32[128]{0:T(128)S(1)}, u32[128]{0:T(128)}, u32[]{:S(2)}) copy-start(u32[128]{0:T(128)} %constant.190) | copy-start | bytes 1540
  42.3 114.1 %copy-start.2 = (bf16[2,512,4,128]{3,1,2,0:T(8,128)(2,1)}, bf16[2,512,4,128]{3,1,2,0:T(8,128)(2,1)S(1)}, u32[]{:S(2)}) copy-start(bf16[2,512,4,128]{3,1,2,0:T(8,128)(2,1)S(1)} %get-tuple-element.1359) | copy-start | bytes 3145732
  43.0 160.7 %all-gather.11.cloned.1.call-start = ((), (), s32[]{:S(2)}) async-start(), calls=%async_computation.5 | async-start | bytes 2228224 | tf_op jit(solution)/shard_map/all_gather | solution.py:13
  168.1 54.8 %copy-start = (f32[2,4,512]{1,2,0:T(8,128)}, f32[2,4,512]{1,2,0:T(8,128)S(1)}, u32[]{:S(2)}) copy-start(f32[2,4,512]{1,2,0:T(8,128)S(1)} %get-tuple-element.1358) | copy-start | bytes 49156
  168.8 52.0 %copy-start.8 = (f32[2,4,128,128]{3,2,1,0:T(8,128)S(1)}, f32[2,4,128,128]{3,2,1,0:T(8,128)}, u32[]{:S(2)}) copy-start(f32[2,4,128,128]{3,2,1,0:T(8,128)} %get-tuple-element.530) | copy-start | bytes 1572868
  168.8 171.7 %reduce-scatter.2.cloned.1.call-start = ((), (), s32[]{:S(2)}) async-start(), calls=%async_computation.3 | async-start | bytes 4456448 | tf_op jit(solution)/shard_map/reduce_scatter | solution.py:204
  225.7 4.4 %copy-start.1 = (bf16[1,512,4,128]{3,2,1,0:T(4,128)(2,1)}, bf16[1,512,4,128]{3,2,1,0:T(4,128)(2,1)S(1)}, u32[]{:S(2)}) copy-start(bf16[1,512,4,128]{3,2,1,0:T(4,128)(2,1)S(1)} %get-tuple-element.1123) | copy-start | bytes 1572868 | tf_op jit(solution)/shard_map/while
  227.1 3.0 copy-start.10
  227.2 2.9 copy-start.5
  227.2 2.9 copy-start.4
  235.1 4.5 %copy-start.6 = (pred[512,512]{1,0:T(8,128)(4,1)S(1)}, pred[512,512]{1,0:T(8,128)(4,1)}, u32[]{:S(2)}) copy-start(pred[512,512]{1,0:T(8,128)(4,1)} %copy-done.5) | copy-start | bytes 786436 | tf_op jit(solution)/shard_map/while
  244.8 4.5 %copy-start.1 = (bf16[1,512,4,128]{3,2,1,0:T(4,128)(2,1)}, bf16[1,512,4,128]{3,2,1,0:T(4,128)(2,1)S(1)}, u32[]{:S(2)}) copy-start(bf16[1,512,4,128]{3,2,1,0:T(4,128)(2,1)S(1)} %get-tuple-element.1123) | copy-start | bytes 1572868 | tf_op jit(solution)/shard_map/while
  246.3 3.0 copy-start.10
  246.4 3.0 copy-start.5
  246.4 3.0 copy-start.4
  254.3 4.5 %copy-start.6 = (pred[512,512]{1,0:T(8,128)(4,1)S(1)}, pred[512,512]{1,0:T(8,128)(4,1)}, u32[]{:S(2)}) copy-start(pred[512,512]{1,0:T(8,128)(4,1)} %copy-done.5) | copy-start | bytes 786436 | tf_op jit(solution)/shard_map/while
  316.3 4.9 %copy-start.7 = (bf16[2,512,4,128]{3,2,1,0:T(4,128)(2,1)S(1)}, bf16[2,512,4,128]{3,2,1,0:T(4,128)(2,1)}, u32[]{:S(2)}) copy-start(bf16[2,512,4,128]{3,2,1,0:T(4,128)(2,1)} %get-tuple-element.532) | copy-start | bytes 3145732
Sparse Core Ops, SparseCore 0:
  9.7 121.9 all-gather.6
  133.3 33.8 all-gather.8
  169.0 34.7 all-gather.10
  272.9 67.5 reduce-scatter.1
